TPU v7x, 32 devices: a whole 2x2x4 slice. The times are simulated.
32 devices in a mesh: seq: 8 (over z, y), tp: 4 (over x, core).
Axes of the slice: x: 2, y: 2, z: 4, core: 2. Of those that a mesh axis runs over, the one named last changes fastest.
Arguments:
- tokens: bfloat16 [8192, 1152], P('seq', 'tp'), may hold values from -6 to 6
- out_grad: bfloat16 [8192, 1152], P('seq', 'tp'), may hold values from -6 to 6
- route_mask: int32 [8192], P('seq'), may hold values from 0 to 1, as said below
- kept_counts: int32 [32], replicated, may hold values from 64 to 192, as said below
- labels: int32 [32], replicated, may hold values from 0 to 1000
- timesteps: int32 [32], replicated, may hold values from 0 to 999
- class_table: bfloat16 [1001, 1152], replicated, may hold values from -6 to 6
- ada_weight: bfloat16 [1152, 6, 1152], P(None, None, 'tp'), may hold values from -0.1875 to 0.1875
- ada_bias: bfloat16 [6, 1152], P(None, 'tp'), may hold values from -2 to 2
- qkv_weight: bfloat16 [1152, 3, 1152], P(None, None, 'tp'), may hold values from -0.1875 to 0.1875
- qv_bias: bfloat16 [2, 1152], P(None, 'tp'), may hold values from -2 to 2
- proj_weight: bfloat16 [1152, 1152], P('tp'), may hold values from -0.5 to 0.5
- proj_bias: bfloat16 [1152], P('tp'), may hold values from -2 to 2
- hidden_weight: bfloat16 [1152, 4608], P(None, 'tp'), may hold values from -0.1875 to 0.1875
- hidden_bias: bfloat16 [4608], P('tp'), may hold values from -2 to 2
- output_weight: bfloat16 [4608, 1152], P('tp'), may hold values from -0.09375 to 0.09375
- output_bias: bfloat16 [1152], P('tp'), may hold values from -2 to 2
Outputs:
- output: bfloat16 [8192, 1152], P('seq', 'tp')
- tokens_grad: bfloat16 [8192, 1152], P('seq', 'tp')
- class_grad: float32 [1001, 1152], P(None, 'seq')
- ada_weight_grad: float32 [1152, 6, 1152], P('seq', None, 'tp')
- ada_bias_grad: float32 [6, 1152], P(None, 'tp')
- qkv_weight_grad: float32 [1152, 3, 1152], P('seq', None, 'tp')
- qv_bias_grad: float32 [2, 1152], P(None, 'tp')
- proj_weight_grad: float32 [1152, 1152], P('tp', 'seq')
- proj_bias_grad: float32 [1152], P('tp')
- hidden_weight_grad: float32 [1152, 4608], P('seq', 'tp')
- hidden_bias_grad: float32 [4608], P('tp')
- output_weight_grad: float32 [4608, 1152], P('tp', 'seq')
- output_bias_grad: float32 [1152], P('tp')
Inputs may be any that keep to these rules, and one draw needn't show every extreme that they name: route_mask keeps exactly kept_counts[i] of the 256 tokens of image i. The kept tokens of all images number 512 * 8; the kept tokens of the first j * 4 images exceed j * 512 by 0 to 128 for every j, by exactly 128 for some j, and by 0 at the end. Every aligned block of 4 images has one image with 192 kept tokens. `route_mask`: consistent with kept_counts.
All inputs are finite; a program needn't handle non-finite values.
Results may differ from a plain program's by a relative error of at most 0.025.
The roundings to bfloat16 on the way count: a program that leaves them out, or rounds other values in their place, can miss the bound.
Values may be sent and summed in bfloat16 or wider, within the bound.
A program may use at most 192 MiB of HBM per device.

v0:
```python
import math

import jax
import jax.numpy as jnp
from jax import lax
from jax.sharding import PartitionSpec as P

HEAD_DIM = 72
IMG_DEV = 4
KEEP_MOST = 192
K_ROWS = 512
SPILL = 128


NORM_EPS = 1e-06
HIGHEST = lax.Precision.HIGHEST


def passed_along(array, axis, by):
    devices = lax.axis_size(axis)
    pairs = [(i, i + by) for i in range(devices) if 0 <= i + by < devices]
    return lax.ppermute(array, axis, pairs)


def padded(array, sides, width):
    for axis, dim in sides:
        devices, length = (lax.axis_size(axis), array.shape[dim])
        up = [(i, (i + 1) % devices) for i in range(devices - 1)]
        down = [(j, i) for i, j in up]
        last = lax.slice_in_dim(array, length - width, length, axis=dim)
        first = lax.slice_in_dim(array, 0, width, axis=dim)
        before = lax.ppermute(last, axis, up)
        after = lax.ppermute(first, axis, down)
        array = jnp.concatenate([before, array, after], axis=dim)
    return array


def exact_dot(left_mat, right_mat):
    return jnp.dot(left_mat, right_mat, precision=HIGHEST, preferred_element_type=jnp.float32)


def time_embed(step_ids, model_width):
    half_width = model_width // 2
    frequency = jnp.exp(-math.log(10000.0) * jnp.arange(half_width, dtype=jnp.float32) / half_width)
    angles = step_ids.astype(jnp.float32)[:, None] * frequency[None, :]
    return jnp.concatenate([jnp.cos(angles), jnp.sin(angles)], axis=1)


def norm_rows(values):
    centered = values - jnp.mean(values, axis=1, keepdims=True)
    inverse = lax.rsqrt(jnp.mean(centered * centered, axis=1, keepdims=True) + NORM_EPS)
    return (centered * inverse, inverse)


def gelu_tanh(values):
    return jax.nn.gelu(values, approximate=True)


def local(
    tokens,
    out_grad,
    route_mask,
    kept_counts,
    labels,
    timesteps,
    class_table,
    ada_weight,
    ada_bias,
    qkv_weight,
    qv_bias,
    proj_weight,
    proj_bias,
    hidden_weight,
    hidden_bias,
    output_weight,
    output_bias,
):
    seq_index = lax.axis_index("seq")
    col_local = tokens.shape[1]
    model_width = class_table.shape[1]
    head_cols = qkv_weight.shape[2]
    heads_local = head_cols // HEAD_DIM
    window_imgs = 2 * IMG_DEV
    block_rows = min(512, K_ROWS)
    span_rows = block_rows + 2 * KEEP_MOST
    scale_factor = HEAD_DIM ** (-0.5)
    col_start = lax.axis_index("tp") * col_local
    image_ends = jnp.cumsum(kept_counts)
    first_image = seq_index * IMG_DEV
    before = jnp.where(seq_index > 0, image_ends[jnp.maximum(first_image - 1, 0)], 0)
    own_total = image_ends[first_image + IMG_DEV - 1] - before
    carry_in = before - seq_index * K_ROWS
    order_idx = jnp.argsort(1 - route_mask, stable=True)[: K_ROWS + SPILL]
    token_rank = jnp.clip(jnp.cumsum(route_mask) - 1, 0, K_ROWS + SPILL - 1)
    kept_flag = route_mask[:, None] > 0
    positions = seq_index * K_ROWS - KEEP_MOST + jnp.arange(K_ROWS + 2 * KEEP_MOST, dtype=jnp.int32)
    image_of = jnp.sum((image_ends[None, :] <= positions[:, None]).astype(jnp.int32), axis=1)
    key_image = jnp.where((positions >= 0) & (positions < image_ends[-1]), image_of, -1)
    row_image = key_image[KEEP_MOST : KEEP_MOST + K_ROWS]
    win_start = jnp.maximum(seq_index - 1, 0) * IMG_DEV
    row_onehot = (
        row_image[:, None] - win_start == jnp.arange(window_imgs, dtype=jnp.int32)[None, :]
    ).astype(jnp.float32)

    def regroup(compact):
        tail_rows = lax.dynamic_slice_in_dim(compact, own_total - SPILL, SPILL, 0)
        arrived = passed_along(tail_rows, "seq", 1)
        joined = jnp.concatenate([arrived, compact], axis=0)
        return lax.dynamic_slice_in_dim(joined, SPILL - carry_in, K_ROWS, 0)

    def reinsert(rows_new, initial):
        arrived = passed_along(rows_new[:SPILL], "seq", -1)
        joined = jnp.concatenate([rows_new, arrived, jnp.zeros_like(arrived)], axis=0)
        compact = lax.dynamic_slice_in_dim(joined, carry_in, K_ROWS + SPILL, 0)
        return jnp.where(kept_flag, compact[token_rank], initial)

    def whole_rows(part_rows):
        return lax.all_gather(part_rows, "tp", axis=1, tiled=True)

    def column_sum(part_rows):
        return lax.psum_scatter(
            part_rows.astype(jnp.bfloat16), "tp", scatter_dimension=1, tiled=True
        ).astype(jnp.float32)

    def own_cols(full_rows):
        return lax.dynamic_slice_in_dim(full_rows, col_start, col_local, 1)

    def input_grads(partial_rows, normed, inverse, scale):
        own_grad = lax.psum_scatter(
            partial_rows.astype(jnp.bfloat16), "tp", scatter_dimension=1, tiled=True
        ).astype(jnp.float32)
        normed_own = own_cols(normed)
        scaled_grad = own_grad * (1.0 + own_cols(scale))
        mean_grad, mean_cross = lax.psum(
            (
                jnp.sum(scaled_grad, axis=1, keepdims=True) / model_width,
                jnp.sum(scaled_grad * normed_own, axis=1, keepdims=True) / model_width,
            ),
            "tp",
        )
        return (
            own_grad,
            own_grad * normed_own,
            inverse * (scaled_grad - mean_grad - normed_own * mean_cross),
        )

    win_labels = lax.dynamic_slice_in_dim(labels, win_start, window_imgs)
    win_steps = lax.dynamic_slice_in_dim(timesteps, win_start, window_imgs)
    label_hot = (
        win_labels[:, None] == jnp.arange(class_table.shape[0], dtype=jnp.int32)[None, :]
    ).astype(jnp.bfloat16)
    condition = jnp.dot(label_hot, class_table, preferred_element_type=jnp.float32) + time_embed(
        win_steps, model_width
    )
    cond_low = jax.nn.silu(condition).astype(jnp.bfloat16)
    mod_own = (
        jnp.dot(
            cond_low,
            ada_weight.reshape(model_width, 6 * col_local),
            preferred_element_type=jnp.float32,
        ).reshape(window_imgs, 6, col_local)
        + ada_bias.astype(jnp.float32)[None]
    )
    mod_full = lax.all_gather(mod_own, "tp", axis=2, tiled=True)

    def row_full(stretch_id):
        return exact_dot(row_onehot, mod_full[:, stretch_id, :])

    def row_own(stretch_id):
        return exact_dot(row_onehot, mod_own[:, stretch_id, :])

    rows_in = regroup(tokens[order_idx])
    full_in = whole_rows(rows_in).astype(jnp.float32)
    normed_one, inverse_one = norm_rows(full_in)
    scale_one = row_full(1)
    branch_one = (normed_one * (1.0 + scale_one) + row_full(0)).astype(jnp.bfloat16)
    qkv_bias = jnp.stack([qv_bias[0], jnp.zeros_like(qv_bias[0]), qv_bias[1]]).astype(jnp.float32)
    qkv_rows = (
        jnp.einsum("rd,dcf->rcf", branch_one, qkv_weight, preferred_element_type=jnp.float32)
        + qkv_bias[None]
    ).astype(jnp.bfloat16)
    query_all = qkv_rows[:, 0].reshape(K_ROWS, heads_local, HEAD_DIM)
    window = padded(qkv_rows[:, 1:], (("seq", 0),), KEEP_MOST)
    window_keys = window[:, 0].reshape(-1, heads_local, HEAD_DIM)
    window_vals = window[:, 1].reshape(-1, heads_local, HEAD_DIM)

    def block_scores(block_index):
        start = block_index * block_rows
        raw = (
            jnp.einsum("qhe,khe->hqk", query_all, window_keys, preferred_element_type=jnp.float32)
            * scale_factor
        )
        same_image = (
            row_image[start : start + block_rows, None]
            == key_image[None, start : start + span_rows]
        )
        return jnp.where(same_image[None], raw, -1e30)

    block_index = 0
    start = block_index * block_rows
    masked = block_scores(block_index)
    top_score = jnp.max(masked, axis=2, keepdims=True)
    exp_scores = jnp.exp(masked - top_score)
    row_total = jnp.sum(exp_scores, axis=2, keepdims=True)
    attn_probs = (exp_scores / row_total).astype(jnp.bfloat16)
    lse_parts = [top_score + jnp.log(row_total)]
    attended_parts = jnp.einsum(
        "hqk,khe->qhe", attn_probs, window_vals, preferred_element_type=jnp.float32
    )
    attended = attended_parts.reshape(K_ROWS, head_cols).astype(jnp.bfloat16)
    attn_out = column_sum(
        jnp.dot(attended, proj_weight, preferred_element_type=jnp.float32)
    ) + proj_bias.astype(jnp.float32)
    gate_one = row_own(2)
    middle = rows_in.astype(jnp.float32) + gate_one * attn_out
    middle_full = whole_rows(middle.astype(jnp.bfloat16)).astype(jnp.float32)
    normed_two, inverse_two = norm_rows(middle_full)
    scale_two = row_full(4)
    branch_two = (normed_two * (1.0 + scale_two) + row_full(3)).astype(jnp.bfloat16)
    pre_act = jnp.dot(
        branch_two, hidden_weight, preferred_element_type=jnp.float32
    ) + hidden_bias.astype(jnp.float32)
    act_low = gelu_tanh(pre_act).astype(jnp.bfloat16)
    mlp_out = column_sum(
        jnp.dot(act_low, output_weight, preferred_element_type=jnp.float32)
    ) + output_bias.astype(jnp.float32)
    gate_two = row_own(5)
    final_rows = middle + gate_two * mlp_out
    output = reinsert(final_rows.astype(jnp.bfloat16), tokens)
    grad_rows = regroup(out_grad[order_idx]).astype(jnp.float32)
    gate_two_rows = grad_rows * mlp_out
    mlp_grad = (grad_rows * gate_two).astype(jnp.bfloat16)
    output_bias_term = jnp.sum(mlp_grad, axis=0, dtype=jnp.float32)
    mlp_grad_full = whole_rows(mlp_grad)
    output_weight_term = jnp.einsum(
        "rf,rd->fd", act_low, mlp_grad_full, preferred_element_type=jnp.float32
    )
    act_grad = jnp.einsum(
        "rd,fd->rf", mlp_grad_full, output_weight, preferred_element_type=jnp.float32
    )
    gelu_pull = jax.vjp(gelu_tanh, pre_act)[1]
    pre_grad = gelu_pull(act_grad)[0].astype(jnp.bfloat16)
    hidden_bias_term = jnp.sum(pre_grad, axis=0, dtype=jnp.float32)
    hidden_weight_term = jnp.einsum(
        "rd,rf->df", branch_two, pre_grad, preferred_element_type=jnp.float32
    )
    two_partial = jnp.einsum(
        "rf,df->rd", pre_grad, hidden_weight, preferred_element_type=jnp.float32
    )
    shift_two_grad, scale_two_grad, two_norm_grad = input_grads(
        two_partial, normed_two, inverse_two, scale_two
    )
    middle_grad = grad_rows + two_norm_grad
    gate_one_rows = middle_grad * attn_out
    attn_grad = (middle_grad * gate_one).astype(jnp.bfloat16)
    proj_bias_term = jnp.sum(attn_grad, axis=0, dtype=jnp.float32)
    attn_grad_full = whole_rows(attn_grad)
    proj_weight_term = jnp.einsum(
        "rf,rd->fd", attended, attn_grad_full, preferred_element_type=jnp.float32
    )
    attended_grad = (
        jnp.einsum("rd,fd->rf", attn_grad_full, proj_weight, preferred_element_type=jnp.float32)
        .astype(jnp.bfloat16)
        .reshape(K_ROWS, heads_local, HEAD_DIM)
    )
    window_grad = jnp.zeros((K_ROWS + 2 * KEEP_MOST, 2, heads_local, HEAD_DIM), jnp.float32)
    block_index = 0
    start = block_index * block_rows
    masked = block_scores(block_index)
    attn_probs = jnp.exp(masked - lse_parts[block_index])
    value_term = jnp.einsum(
        "hqk,qhe->khe",
        attn_probs.astype(jnp.bfloat16),
        attended_grad,
        preferred_element_type=jnp.float32,
    )
    prob_grad = jnp.einsum(
        "qhe,khe->hqk", attended_grad, window_vals, preferred_element_type=jnp.float32
    )
    row_dot = jnp.sum(attn_probs * prob_grad, axis=2, keepdims=True)
    score_grad = (attn_probs * (prob_grad - row_dot)).astype(jnp.bfloat16)
    query_parts = (
        jnp.einsum("hqk,khe->qhe", score_grad, window_keys, preferred_element_type=jnp.float32)
        * scale_factor
    )
    key_term = (
        jnp.einsum("hqk,qhe->khe", score_grad, query_all, preferred_element_type=jnp.float32)
        * scale_factor
    )
    window_grad = window_grad.at[start : start + span_rows].add(
        jnp.stack([key_term, value_term], axis=1)
    )
    from_right = passed_along(window_grad[:KEEP_MOST].astype(jnp.bfloat16), "seq", -1).astype(
        jnp.float32
    )
    from_left = passed_along(
        window_grad[K_ROWS + KEEP_MOST :].astype(jnp.bfloat16), "seq", 1
    ).astype(jnp.float32)
    own_kv = window_grad[KEEP_MOST : KEEP_MOST + K_ROWS]
    own_kv = own_kv.at[:KEEP_MOST].add(from_left).at[K_ROWS - KEEP_MOST :].add(from_right)
    qkv_grad = (
        jnp.concatenate([query_parts[:, None], own_kv], axis=1)
        .reshape(K_ROWS, 3, head_cols)
        .astype(jnp.bfloat16)
    )
    qkv_sums = jnp.sum(qkv_grad, axis=0, dtype=jnp.float32)
    qv_bias_term = jnp.stack([qkv_sums[0], qkv_sums[2]])
    qkv_weight_term = jnp.einsum(
        "rd,rcf->dcf", branch_one, qkv_grad, preferred_element_type=jnp.float32
    )
    one_partial = jnp.einsum(
        "rcf,dcf->rd", qkv_grad, qkv_weight, preferred_element_type=jnp.float32
    )
    shift_one_grad, scale_one_grad, one_norm_grad = input_grads(
        one_partial, normed_one, inverse_one, scale_one
    )
    in_grad = middle_grad + one_norm_grad
    tokens_grad = reinsert(in_grad.astype(jnp.bfloat16), out_grad)
    per_row = jnp.stack(
        [
            shift_one_grad,
            scale_one_grad,
            gate_one_rows,
            shift_two_grad,
            scale_two_grad,
            gate_two_rows,
        ],
        axis=1,
    )
    mod_grad = jnp.einsum(
        "rw,rcf->wcf", row_onehot, per_row, precision=HIGHEST, preferred_element_type=jnp.float32
    )
    ada_bias_term = jnp.sum(mod_grad, axis=0)
    ada_weight_term = jnp.einsum(
        "wd,wcf->dcf",
        cond_low.astype(jnp.float32),
        mod_grad,
        precision=HIGHEST,
        preferred_element_type=jnp.float32,
    )
    cond_grad = lax.psum(
        jnp.einsum(
            "wcf,dcf->wd",
            mod_grad,
            ada_weight.astype(jnp.float32),
            precision=HIGHEST,
            preferred_element_type=jnp.float32,
        ).astype(jnp.bfloat16),
        "tp",
    ).astype(jnp.float32)
    silu_pull = jax.vjp(jax.nn.silu, condition)[1]
    class_term = jnp.einsum(
        "wc,wd->cd",
        label_hot.astype(jnp.float32),
        silu_pull(cond_grad)[0],
        precision=HIGHEST,
        preferred_element_type=jnp.float32,
    )
    (
        ada_weight_grad,
        qkv_weight_grad,
        proj_weight_grad,
        hidden_weight_grad,
        output_weight_grad,
        class_grad,
    ) = (
        lax.psum_scatter(ada_weight_term, "seq", scatter_dimension=0, tiled=True),
        lax.psum_scatter(qkv_weight_term, "seq", scatter_dimension=0, tiled=True),
        lax.psum_scatter(proj_weight_term, "seq", scatter_dimension=1, tiled=True),
        lax.psum_scatter(hidden_weight_term, "seq", scatter_dimension=0, tiled=True),
        lax.psum_scatter(output_weight_term, "seq", scatter_dimension=1, tiled=True),
        lax.psum_scatter(class_term, "seq", scatter_dimension=1, tiled=True),
    )
    ada_bias_grad, qv_bias_grad, proj_bias_grad, hidden_bias_grad, output_bias_grad = lax.psum(
        (ada_bias_term, qv_bias_term, proj_bias_term, hidden_bias_term, output_bias_term), "seq"
    )
    return (
        output,
        tokens_grad,
        class_grad,
        ada_weight_grad,
        ada_bias_grad,
        qkv_weight_grad,
        qv_bias_grad,
        proj_weight_grad,
        proj_bias_grad,
        hidden_weight_grad,
        hidden_bias_grad,
        output_weight_grad,
        output_bias_grad,
    )


def solution(mesh):
    return jax.shard_map(
        local,
        mesh=mesh,
        in_specs=(
            P("seq", "tp"),
            P("seq", "tp"),
            P("seq"),
            P(),
            P(),
            P(),
            P(),
            P(None, None, "tp"),
            P(None, "tp"),
            P(None, None, "tp"),
            P(None, "tp"),
            P("tp", None),
            P("tp"),
            P(None, "tp"),
            P("tp"),
            P("tp", None),
            P("tp"),
        ),
        out_specs=(
            P("seq", "tp"),
            P("seq", "tp"),
            P(None, "seq"),
            P("seq", None, "tp"),
            P(None, "tp"),
            P("seq", None, "tp"),
            P(None, "tp"),
            P("tp", "seq"),
            P("tp"),
            P("seq", "tp"),
            P("tp"),
            P("tp", "seq"),
            P("tp"),
        ),
        check_vma=False,
    )
```

profile of v0, /device:TPU:0, one launch (start us, length us, event | category | flops | bytes accessed | tf_op | source)
XLA Modules:
  0.0 1055.8 jit_solution(1580755687282485058)
XLA Ops:
  25.2 5.5 collective-permute-start
  38.7 39.6 %all_gather.16 = f32[8,6,1152]{1,0,2:T(8,128)} all-gather(f32[8,6,288]{1,0,2:T(8,128)} %copy.132), channel_id=1, replica_groups=mesh['seq'=8,'tp'=4] {'tp'}, dimensions={2}, use_global_device_ids=true | all-gather | bytes 276480 | tf_op jit(solution)/shard_map/all_gather | solution.py:164
  79.3 15.2 %fusion.94 = (f32[8,1,1152]{1,0,2:T(8,128)}, f32[8,1,1152]{1,0,2:T(8,128)}, f32[8,1,1152]{1,0,2:T(8,128)}, f32[8,1,1152]{1,0,2:T(8,128)}) fusion(f32[8,6,1152]{1,0,2:T(8,128)} %all_gather.16), kind=kLoop, calls=%fused_computation.195 | loop fusion | bytes 294912 | tf_op jit(solution)/shard_map/slice | solution.py:167
  124.7 11.1 %collective-permute-done.1 = bf16[192,2,288]{0,2,1:T(8,128)(2,1)S(1)} collective-permute-done((bf16[192,2,288]{0,2,1:T(8,128)(2,1)S(1)}, bf16[192,2,288]{0,2,1:T(8,128)(2,1)S(1)}, u32[]{:S(2)}, u32[]{:S(2)}) %collective-permute-start.1) | collective-permute-done | bytes 221216 | tf_op jit(solution)/shard_map/ppermute | solution.py:32
  147.3 25.8 %reduce-scatter.11.cloned.1.call-done = bf16[512,288]{0,1:T(8,128)(2,1)} async-done(((bf16[512,1152]{0,1:T(8,128)(2,1)}), bf16[512,288]{0,1:T(8,128)(2,1)}) %reduce-scatter.11.cloned.1.call-update) | async-done | bytes 294928 | tf_op jit(solution)/shard_map/reduce_scatter | solution.py:121
  218.2 5.9 convert_reduce_fusion.2
  235.9 17.8 %reduce-scatter.15.cloned.1.call-done = bf16[512,288]{0,1:T(8,128)(2,1)} async-done(((bf16[512,1152]{0,1:T(8,128)(2,1)}), bf16[512,288]{0,1:T(8,128)(2,1)}) %reduce-scatter.15.cloned.1.call-update) | async-done | bytes 294928 | tf_op jit(solution)/shard_map/reduce_scatter | solution.py:129
  255.0 5.8 all-reduce.2
  260.8 21.1 %reduce-scatter.13.cloned.1.call-done = bf16[512,288]{0,1:T(8,128)(2,1)} async-done(((bf16[512,1152]{0,1:T(8,128)(2,1)}), bf16[512,288]{0,1:T(8,128)(2,1)}) %reduce-scatter.13.cloned.1.call-update) | async-done | bytes 294928 | tf_op jit(solution)/shard_map/reduce_scatter | solution.py:121
  285.4 17.4 %all-gather.11.cloned.1.call-done = bf16[512,1152]{0,1:T(8,128)(2,1)} async-done(((bf16[512,288]{0,1:T(8,128)(2,1)}), bf16[512,1152]{0,1:T(8,128)(2,1)}) %all-gather.11.cloned.1.call-update) | async-done | bytes 1179664 | tf_op jit(solution)/shard_map/all_gather | solution.py:118
  309.4 4.6 multiply_reduce_fusion
  346.8 6.1 fusion.90
  354.2 5.3 fusion.104
  379.1 10.7 %psum.74 = bf16[8,1152]{1,0:T(8,128)(2,1)S(1)} all-reduce(bf16[8,1152]{1,0:T(8,128)(2,1)S(1)} %fusion.25), channel_id=1, replica_groups=mesh['seq'=8,'tp'=4] {'tp'}, use_global_device_ids=true, to_apply=%region_24.25 | all-reduce | flops 9216 | bytes 36864 | tf_op jit(solution)/shard_map/psum | solution.py:341
  394.2 7.0 fusion.69
  407.9 6.3 all-reduce.1
  417.8 42.5 %all-reduce = (f32[6,288]{1,0:T(8,128)}, f32[2,288]{1,0:T(2,128)}, f32[288]{0:T(512)}, f32[1152]{0:T(1024)}, f32[288]{0:T(512)}) all-reduce(f32[6,288]{1,0:T(8,128)S(1)} %get-tuple-element.178, f32[2,288]{1,0:T(2,128)S(1)} %pad_maximum_fusion.5, f32[288]{0:T(512)S(1)} %get-tuple-element.142, ...), channel_id=1, replica_groups=mesh['seq'=8,'tp'=4] {'seq'}, use_global_device_ids=true, to_apply=%region_28.29 | all-reduce | flops 4032 | bytes 32256 | tf_op jit(solution)/shard_map/psum | solution.py:374
  462.6 5.0 gather_fusion.3
  467.5 5.0 gather_fusion.1
  480.3 69.1 %reduce-scatter.29.cloned.1.call-done = f32[1152,144]{0,1:T(8,128)} async-done(((f32[1152,1152]{0,1:T(8,128)}), f32[1152,144]{0,1:T(8,128)}) %reduce-scatter.29.cloned.1.call-update) | async-done | bytes 663568 | tf_op jit(solution)/shard_map/reduce_scatter | solution.py:371
  549.4 108.1 %reduce-scatter.27.cloned.1.call-done = f32[144,1152]{1,0:T(8,128)} async-done(((f32[1152,1152]{1,0:T(8,128)}), f32[144,1152]{1,0:T(8,128)}) %reduce-scatter.27.cloned.1.call-update) | async-done | bytes 663568 | tf_op jit(solution)/shard_map/reduce_scatter | solution.py:370
  657.5 108.3 %reduce-scatter.23.cloned.1.call-done = f32[144,3,288]{2,0,1:T(8,128)} async-done(((f32[1152,3,288]{2,0,1:T(8,128)}), f32[144,3,288]{2,0,1:T(8,128)}) %reduce-scatter.23.cloned.1.call-update) | async-done | bytes 497680 | tf_op jit(solution)/shard_map/reduce_scatter | solution.py:368
  765.8 99.3 %reduce-scatter.19.cloned.1.call-done = f32[1001,144]{0,1:T(8,128)} async-done(((f32[1001,1152]{0,1:T(8,128)}), f32[1001,144]{0,1:T(8,128)}) %reduce-scatter.19.cloned.1.call-update) | async-done | bytes 576592 | tf_op jit(solution)/shard_map/reduce_scatter | solution.py:372
  865.1 183.8 %reduce-scatter.21.cloned.1.call-done = f32[144,6,288]{2,0,1:T(8,128)} async-done(((f32[1152,6,288]{2,0,1:T(8,128)}), f32[144,6,288]{2,0,1:T(8,128)}) %reduce-scatter.21.cloned.1.call-update) | async-done | bytes 995344 | tf_op jit(solution)/shard_map/reduce_scatter | solution.py:367
  (316 shorter events, 213.1 us)
Async XLA Ops:
  7.2 211.0 %copy-start = (bf16[1152,1152]{1,0:T(8,128)(2,1)S(1)}, bf16[1152,1152]{1,0:T(8,128)(2,1)}, u32[]{:S(2)}) copy-start(bf16[1152,1152]{1,0:T(8,128)(2,1)} %param.40) | copy-start | bytes 7962628
  7.2 103.1 %all-gather.5.cloned.1.call-start = ((), (), s32[]{:S(2)}) async-start(), calls=%async_computation.10 | async-start | bytes 1474560 | tf_op jit(solution)/shard_map/all_gather | solution.py:118
  25.2 53.1 %collective-permute-start = (bf16[128,288]{0,1:T(8,128)(2,1)}, bf16[128,288]{0,1:T(8,128)(2,1)}, u32[]{:S(2)}, u32[]{:S(2)}) collective-permute-start(bf16[128,288]{0,1:T(8,128)(2,1)} %constant_dynamic-slice_fusion.1), channel_id=1, source_target_pairs={{0,4},{4,8},{8,12},{12,16},{16,20},{20,24},{24,28},{1,5},{5,9},{9,... | collective-permute-start | bytes 221192 | tf_op jit(solution)/shard_map/ppermute | solution.py:22
  79.2 93.8 %reduce-scatter.11.cloned.1.call-start = ((), (), s32[]{:S(2)}) async-start(), calls=%async_computation.11 | async-start | bytes 1474560 | tf_op jit(solution)/shard_map/reduce_scatter | solution.py:121
  119.0 16.8 %collective-permute-start.1 = (bf16[192,2,288]{0,2,1:T(8,128)(2,1)S(1)}, bf16[192,2,288]{0,2,1:T(8,128)(2,1)S(1)}, u32[]{:S(2)}, u32[]{:S(2)}) collective-permute-start(bf16[192,2,288]{0,2,1:T(8,128)(2,1)S(1)} %get-tuple-element.153), channel_id=1, source_target_pairs={{0,4},{4,8},{8,12},{12,16},{16,20},{20,24},{24,28},{1,5},{5,9},{9,... | collective-permute-start | bytes 663560 | tf_op jit(solution)/shard_map/ppermute | solution.py:32
  123.0 12.9 %collective-permute-start.2 = (bf16[192,2,288]{0,2,1:T(8,128)(2,1)S(1)}, bf16[192,2,288]{0,2,1:T(8,128)(2,1)S(1)}, u32[]{:S(2)}, u32[]{:S(2)}) collective-permute-start(bf16[192,2,288]{0,2,1:T(8,128)(2,1)S(1)} %get-tuple-element.154), channel_id=1, source_target_pairs={{4,0},{8,4},{12,8},{16,12},{20,16},{24,20},{28,24},{5,1},{9,5},{13... | collective-permute-start | bytes 663560 | tf_op jit(solution)/shard_map/ppermute | solution.py:33
  146.0 59.9 %all-gather.7.cloned.1.call-start = ((), (), s32[]{:S(2)}) async-start(), calls=%async_computation.12 | async-start | bytes 1474560 | tf_op jit(solution)/shard_map/all_gather | solution.py:118
  175.6 42.6 %all-gather.9.cloned.1.call-start = ((), (), s32[]{:S(2)}) async-start(), calls=%async_computation.14 | async-start | bytes 1474560 | tf_op jit(solution)/shard_map/all_gather | solution.py:118
  185.9 13.1 %collective-permute-start.4 = (bf16[128,288]{0,1:T(8,128)(2,1)}, bf16[128,288]{0,1:T(8,128)(2,1)}, u32[]{:S(2)}, u32[]{:S(2)}) collective-permute-start(bf16[128,288]{0,1:T(8,128)(2,1)} %constant_dynamic-slice_fusion), channel_id=1, source_target_pairs={{0,4},{4,8},{8,12},{12,16},{16,20},{20,24},{24,28},{1,5},{5,9},{9,... | collective-permute-start | bytes 221192 | tf_op jit(solution)/shard_map/ppermute | solution.py:22
  202.1 51.6 %reduce-scatter.15.cloned.1.call-start = ((), (), s32[]{:S(2)}) async-start(), calls=%async_computation.15 | async-start | bytes 1474560 | tf_op jit(solution)/shard_map/reduce_scatter | solution.py:129
  227.9 54.0 %reduce-scatter.13.cloned.1.call-start = ((), (), s32[]{:S(2)}) async-start(), calls=%async_computation.13 | async-start | bytes 1474560 | tf_op jit(solution)/shard_map/reduce_scatter | solution.py:121
  232.5 70.2 %all-gather.11.cloned.1.call-start = ((), (), s32[]{:S(2)}) async-start(), calls=%async_computation.16 | async-start | bytes 1474560 | tf_op jit(solution)/shard_map/all_gather | solution.py:118
  285.1 86.2 %reduce-scatter.17.cloned.1.call-start = ((), (), s32[]{:S(2)}) async-start(), calls=%async_computation.17 | async-start | bytes 1474560 | tf_op jit(solution)/shard_map/reduce_scatter | solution.py:129
  317.3 10.0 collective-permute-start.5
  322.8 11.1 %collective-permute-start.6 = (bf16[192,2,4,72]{0,3,2,1:T(8,128)(2,1)}, bf16[192,2,4,72]{0,3,2,1:T(8,128)(2,1)}, u32[]{:S(2)}, u32[]{:S(2)}) collective-permute-start(bf16[192,2,4,72]{0,3,2,1:T(8,128)(2,1)} %get-tuple-element.149), channel_id=1, source_target_pairs={{4,0},{8,4},{12,8},{16,12},{20,16},{24,20},{28,24},{5,1},{9,5},{13... | collective-permute-start | bytes 663560 | tf_op jit(solution)/shard_map/ppermute | solution.py:22
  344.6 135.7 %reduce-scatter.25.cloned.1.call-start = ((), (), s32[]{:S(2)}) async-start(), calls=%async_computation.21 | async-start | bytes 1990656 | tf_op jit(solution)/shard_map/reduce_scatter | solution.py:369
  346.7 202.6 %reduce-scatter.29.cloned.1.call-start = ((), (), s32[]{:S(2)}) async-start(), calls=%async_computation.23 | async-start | bytes 5971968 | tf_op jit(solution)/shard_map/reduce_scatter | solution.py:371
  352.9 304.5 %reduce-scatter.27.cloned.1.call-start = ((), (), s32[]{:S(2)}) async-start(), calls=%async_computation.22 | async-start | bytes 5971968 | tf_op jit(solution)/shard_map/reduce_scatter | solution.py:370
  359.6 406.2 %reduce-scatter.23.cloned.1.call-start = ((), (), s32[]{:S(2)}) async-start(), calls=%async_computation.20 | async-start | bytes 5971968 | tf_op jit(solution)/shard_map/reduce_scatter | solution.py:368
  365.0 500.1 %reduce-scatter.19.cloned.1.call-start = ((), (), s32[]{:S(2)}) async-start(), calls=%async_computation.18 | async-start | bytes 5308416 | tf_op jit(solution)/shard_map/reduce_scatter | solution.py:372
  394.1 654.7 %reduce-scatter.21.cloned.1.call-start = ((), (), s32[]{:S(2)}) async-start(), calls=%async_computation.19 | async-start | bytes 11943936 | tf_op jit(solution)/shard_map/reduce_scatter | solution.py:367
  403.3 57.0 %collective-permute-start.3 = (bf16[128,288]{0,1:T(8,128)(2,1)S(1)}, bf16[128,288]{0,1:T(8,128)(2,1)}, u32[]{:S(2)}, u32[]{:S(2)}) collective-permute-start(bf16[128,288]{0,1:T(8,128)(2,1)S(1)} %slice.217), channel_id=1, source_target_pairs={{4,0},{8,4},{12,8},{16,12},{20,16},{24,20},{28,24},{5,1},{9,5},{13... | collective-permute-start | bytes 221192 | tf_op jit(solution)/shard_map/ppermute | solution.py:22
  416.5 43.9 %collective-permute-start.7 = (bf16[128,288]{0,1:T(8,128)(2,1)S(1)}, bf16[128,288]{0,1:T(8,128)(2,1)S(1)}, u32[]{:S(2)}, u32[]{:S(2)}) collective-permute-start(bf16[128,288]{0,1:T(8,128)(2,1)S(1)} %slice.226), channel_id=1, source_target_pairs={{4,0},{8,4},{12,8},{16,12},{20,16},{24,20},{28,24},{5,1},{9,5},{13... | collective-permute-start | bytes 221192 | tf_op jit(solution)/shard_map/ppermute | solution.py:22
  472.6 576.3 %copy-start.1 = (bf16[1152,1152]{1,0:T(8,128)(2,1)S(1)}, bf16[1152,1152]{1,0:T(8,128)(2,1)}, u32[]{:S(2)}) copy-start(bf16[1152,1152]{1,0:T(8,128)(2,1)} %param.40) | copy-start | bytes 7962628
  (70 other events, 512.9 us)
Sparse Core Ops, SparseCore 0:
  79.3 17.1 all-gather.4
  146.1 26.9 reduce-scatter.10
  175.7 17.4 all-gather.6
  202.2 15.9 all-gather.8
  228.0 25.7 reduce-scatter.14
  256.1 25.7 reduce-scatter.12
  285.3 17.4 all-gather.10
  344.7 26.5 reduce-scatter.16
  375.4 66.5 reduce-scatter.24
  446.5 102.8 reduce-scatter.28
  553.5 103.9 reduce-scatter.26
  661.9 103.8 reduce-scatter.22
  770.0 95.0 reduce-scatter.18
  869.1 179.6 reduce-scatter.20
where the time goes:
time: 1070 us; the launch traced here: 1060 us
  waiting for transfers between devices  671 us (63%)
  blocking collectives  105 us (10%)
  matrix products  98.7 us (9%)
  local copies, waits for them, and re-layouts  87.5 us (8%)
  other arithmetic  53.5 us (5%)
  starting transfers between devices  23.5 us (2%)
  between operations  16.7 us (2%)
    reduce_scatter x1, waiting for transfers between devices, local(): lax.psum_scatter(ada_weight_term, 'seq', scatter_dimension=0, tiled=True)  184 us
    reduce_scatter x1, waiting for transfers between devices, local(): lax.psum_scatter(qkv_weight_term, 'seq', scatter_dimension=0, tiled=True)  108 us
    reduce_scatter x1, waiting for transfers between devices, local(): lax.psum_scatter(hidden_weight_term, 'seq', scatter_dimension=0, tiled=True)  108 us
    reduce_scatter x1, waiting for transfers between devices, local(): lax.psum_scatter(class_term, 'seq', scatter_dimension=1, tiled=True)  99.3 us
    reduce_scatter x1, waiting for transfers between devices, local(): lax.psum_scatter(output_weight_term, 'seq', scatter_dimension=1, tiled=True)  69.1 us
    reduce_scatter x2, waiting for transfers between devices, column_sum(): lax.psum_scatter(part_rows.astype(jnp.bfloat16), 'tp', scatter_dimension=...  46.9 us
    psum x1, blocking collectives, local(): lax.psum((ada_bias_term, qv_bias_term, proj_bias_term, hidden_bias_term,...  42.5 us
    all_gather x1, blocking collectives, local(): mod_full = lax.all_gather(mod_own, 'tp', axis=2, tiled=True)  39.6 us
  transfers between devices with their start and end apart: 22, of which 14 were waited for; matrix products, arithmetic and copies ran while one was open for 15% of the time, Pallas kernels for 0%

commit v1 on v0

v1 whole, which is shorter than its diff:
```python
import math

import jax
import jax.numpy as jnp
from jax import lax
from jax.sharding import PartitionSpec as P

HEAD_DIM = 72
IMG_DEV = 4
ROWS = 640


NORM_EPS = 1e-06
HIGHEST = lax.Precision.HIGHEST


def exact_dot(left_mat, right_mat):
    return jnp.dot(left_mat, right_mat, precision=HIGHEST, preferred_element_type=jnp.float32)


def time_embed(step_ids, model_width):
    half_width = model_width // 2
    frequency = jnp.exp(-math.log(10000.0) * jnp.arange(half_width, dtype=jnp.float32) / half_width)
    angles = step_ids.astype(jnp.float32)[:, None] * frequency[None, :]
    return jnp.concatenate([jnp.cos(angles), jnp.sin(angles)], axis=1)


def norm_rows(values):
    centered = values - jnp.mean(values, axis=1, keepdims=True)
    inverse = lax.rsqrt(jnp.mean(centered * centered, axis=1, keepdims=True) + NORM_EPS)
    return (centered * inverse, inverse)


def gelu_tanh(values):
    return jax.nn.gelu(values, approximate=True)


def local(
    tokens,
    out_grad,
    route_mask,
    kept_counts,
    labels,
    timesteps,
    class_table,
    ada_weight,
    ada_bias,
    qkv_weight,
    qv_bias,
    proj_weight,
    proj_bias,
    hidden_weight,
    hidden_bias,
    output_weight,
    output_bias,
):
    f32, bf16 = jnp.float32, jnp.bfloat16
    seq_index = lax.axis_index("seq")
    tp_index = lax.axis_index("tp")
    seq_size = lax.axis_size("seq")
    col_local = tokens.shape[1]
    model_width = class_table.shape[1]
    head_cols = qkv_weight.shape[2]
    heads_local = head_cols // HEAD_DIM
    slice_width = model_width // seq_size
    images = kept_counts.shape[0]
    scale_factor = HEAD_DIM ** (-0.5)
    col_start = tp_index * col_local
    first_image = seq_index * IMG_DEV
    own_counts = lax.dynamic_slice_in_dim(kept_counts, first_image, IMG_DEV)
    own_ends = jnp.cumsum(own_counts)
    rank = jnp.where(route_mask > 0, jnp.cumsum(route_mask) - 1, -1)
    row_ids = jnp.arange(ROWS, dtype=jnp.int32)
    place = (rank[None, :] == row_ids[:, None]).astype(bf16)
    row_image = jnp.sum((own_ends[None, :] <= row_ids[:, None]).astype(jnp.int32), axis=1)
    row_onehot = (row_image[:, None] == jnp.arange(IMG_DEV, dtype=jnp.int32)[None, :]).astype(f32)

    def whole_rows(part_rows):
        return lax.all_gather(part_rows, "tp", axis=1, tiled=True)

    def column_sum(part_rows):
        return lax.psum_scatter(
            part_rows.astype(bf16), "tp", scatter_dimension=1, tiled=True
        ).astype(f32)

    def own_cols(full_rows):
        return lax.dynamic_slice_in_dim(full_rows, col_start, col_local, 1)

    def reinsert(rows_new, initial):
        placed = jnp.einsum("rt,rc->tc", place, rows_new, preferred_element_type=f32).astype(bf16)
        return jnp.where(route_mask[:, None] > 0, placed, initial)

    label_hot = (
        labels[:, None] == jnp.arange(class_table.shape[0], dtype=jnp.int32)[None, :]
    ).astype(bf16)
    condition = jnp.dot(label_hot, class_table, preferred_element_type=f32) + time_embed(
        timesteps, model_width
    )
    cond_low = jax.nn.silu(condition).astype(bf16)
    cond_own = lax.dynamic_slice_in_dim(cond_low, first_image, IMG_DEV)
    mod_own = (
        jnp.einsum("wd,dcf->wcf", cond_own, ada_weight, preferred_element_type=f32)
        + ada_bias.astype(f32)[None]
    )
    mod_full = lax.all_gather(mod_own, "tp", axis=2, tiled=True)

    def row_full(stretch_id):
        return exact_dot(row_onehot, mod_full[:, stretch_id, :])

    def row_own(stretch_id):
        return exact_dot(row_onehot, mod_own[:, stretch_id, :])

    def input_grads(partial_rows, normed, inverse, scale):
        own_grad = column_sum(partial_rows)
        normed_own = own_cols(normed)
        scaled_grad = own_grad * (1.0 + own_cols(scale))
        mean_grad, mean_cross = lax.psum(
            (
                jnp.sum(scaled_grad, axis=1, keepdims=True) / model_width,
                jnp.sum(scaled_grad * normed_own, axis=1, keepdims=True) / model_width,
            ),
            "tp",
        )
        return (
            own_grad,
            own_grad * normed_own,
            inverse * (scaled_grad - mean_grad - normed_own * mean_cross),
        )

    picked = jnp.dot(
        place, jnp.concatenate([tokens, out_grad], axis=1), preferred_element_type=f32
    )
    rows_in = picked[:, :col_local].astype(bf16)
    grad_rows = picked[:, col_local:]
    gate_one = row_own(2)
    gate_two = row_own(5)
    mlp_grad = (grad_rows * gate_two).astype(bf16)
    full_in = whole_rows(rows_in).astype(f32)
    mlp_grad_full = whole_rows(mlp_grad)
    normed_one, inverse_one = norm_rows(full_in)
    scale_one = row_full(1)
    branch_one = (normed_one * (1.0 + scale_one) + row_full(0)).astype(bf16)
    qkv_bias = jnp.stack([qv_bias[0], jnp.zeros_like(qv_bias[0]), qv_bias[1]]).astype(f32)
    qkv_rows = (
        jnp.einsum("rd,dcf->rcf", branch_one, qkv_weight, preferred_element_type=f32)
        + qkv_bias[None]
    ).astype(bf16)
    query_all, key_all, value_all = (
        qkv_rows[:, part].reshape(ROWS, heads_local, HEAD_DIM) for part in range(3)
    )
    same_image = row_image[:, None] == row_image[None, :]
    raw = jnp.einsum("qhe,khe->hqk", query_all, key_all, preferred_element_type=f32) * scale_factor
    masked = jnp.where(same_image[None], raw, -1e30)
    top_score = jnp.max(masked, axis=2, keepdims=True)
    exp_scores = jnp.exp(masked - top_score)
    attn_probs = exp_scores / jnp.sum(exp_scores, axis=2, keepdims=True)
    probs_low = attn_probs.astype(bf16)
    attended = (
        jnp.einsum("hqk,khe->qhe", probs_low, value_all, preferred_element_type=f32)
        .reshape(ROWS, head_cols)
        .astype(bf16)
    )
    attn_out = column_sum(
        jnp.dot(attended, proj_weight, preferred_element_type=f32)
    ) + proj_bias.astype(f32)
    middle = rows_in.astype(f32) + gate_one * attn_out
    middle_full = whole_rows(middle.astype(bf16)).astype(f32)
    normed_two, inverse_two = norm_rows(middle_full)
    scale_two = row_full(4)
    branch_two = (normed_two * (1.0 + scale_two) + row_full(3)).astype(bf16)
    pre_act = jnp.dot(branch_two, hidden_weight, preferred_element_type=f32) + hidden_bias.astype(
        f32
    )
    act_low = gelu_tanh(pre_act).astype(bf16)
    mlp_out = column_sum(
        jnp.dot(act_low, output_weight, preferred_element_type=f32)
    ) + output_bias.astype(f32)
    final_rows = middle + gate_two * mlp_out
    output = reinsert(final_rows.astype(bf16), tokens)
    gate_two_rows = grad_rows * mlp_out
    output_bias_term = jnp.sum(mlp_grad, axis=0, dtype=f32)
    output_weight_term = jnp.einsum(
        "rf,rd->fd", act_low, mlp_grad_full, preferred_element_type=f32
    ).astype(bf16)
    act_grad = jnp.einsum("rd,fd->rf", mlp_grad_full, output_weight, preferred_element_type=f32)
    gelu_pull = jax.vjp(gelu_tanh, pre_act)[1]
    pre_grad = gelu_pull(act_grad)[0].astype(bf16)
    hidden_bias_term = jnp.sum(pre_grad, axis=0, dtype=f32)
    hidden_weight_term = jnp.einsum(
        "rd,rf->df", branch_two, pre_grad, preferred_element_type=f32
    ).astype(bf16)
    two_partial = jnp.einsum("rf,df->rd", pre_grad, hidden_weight, preferred_element_type=f32)
    shift_two_grad, scale_two_grad, two_norm_grad = input_grads(
        two_partial, normed_two, inverse_two, scale_two
    )
    middle_grad = grad_rows + two_norm_grad
    gate_one_rows = middle_grad * attn_out
    attn_grad = (middle_grad * gate_one).astype(bf16)
    proj_bias_term = jnp.sum(attn_grad, axis=0, dtype=f32)
    attn_grad_full = whole_rows(attn_grad)
    proj_weight_term = jnp.einsum(
        "rf,rd->fd", attended, attn_grad_full, preferred_element_type=f32
    ).astype(bf16)
    attended_grad = (
        jnp.einsum("rd,fd->rf", attn_grad_full, proj_weight, preferred_element_type=f32)
        .astype(bf16)
        .reshape(ROWS, heads_local, HEAD_DIM)
    )
    value_term = jnp.einsum("hqk,qhe->khe", probs_low, attended_grad, preferred_element_type=f32)
    prob_grad = jnp.einsum("qhe,khe->hqk", attended_grad, value_all, preferred_element_type=f32)
    row_dot = jnp.sum(attn_probs * prob_grad, axis=2, keepdims=True)
    score_grad = (attn_probs * (prob_grad - row_dot)).astype(bf16)
    query_term = (
        jnp.einsum("hqk,khe->qhe", score_grad, key_all, preferred_element_type=f32) * scale_factor
    )
    key_term = (
        jnp.einsum("hqk,qhe->khe", score_grad, query_all, preferred_element_type=f32)
        * scale_factor
    )
    qkv_grad = (
        jnp.stack([query_term, key_term, value_term], axis=1)
        .reshape(ROWS, 3, head_cols)
        .astype(bf16)
    )
    qkv_sums = jnp.sum(qkv_grad, axis=0, dtype=f32)
    qkv_weight_term = jnp.einsum(
        "rd,rcf->dcf", branch_one, qkv_grad, preferred_element_type=f32
    ).astype(bf16)
    one_partial = jnp.einsum("rcf,dcf->rd", qkv_grad, qkv_weight, preferred_element_type=f32)
    shift_one_grad, scale_one_grad, one_norm_grad = input_grads(
        one_partial, normed_one, inverse_one, scale_one
    )
    in_grad = middle_grad + one_norm_grad
    tokens_grad = reinsert(in_grad.astype(bf16), out_grad)
    per_row = jnp.concatenate(
        [
            shift_one_grad,
            scale_one_grad,
            gate_one_rows,
            shift_two_grad,
            scale_two_grad,
            gate_two_rows,
        ],
        axis=1,
    )
    mod_grad = jnp.einsum(
        "rw,rf->wf", row_onehot, per_row, precision=HIGHEST, preferred_element_type=f32
    )
    small = jnp.concatenate(
        [
            mod_grad.reshape(-1),
            qkv_sums[0],
            qkv_sums[2],
            proj_bias_term,
            hidden_bias_term,
            output_bias_term,
        ]
    )
    small_all = lax.all_gather(small, "seq", axis=0)
    mod_size = mod_grad.size
    mod_all = small_all[:, :mod_size].reshape(images, 6, col_local)
    bias_sums = jnp.sum(small_all[:, mod_size:], axis=0)
    ada_bias_grad = jnp.sum(mod_all, axis=0)
    qv_bias_grad = bias_sums[: 2 * col_local].reshape(2, col_local)
    at = 2 * col_local
    proj_bias_grad = bias_sums[at : at + col_local]
    at += col_local
    hidden_bias_grad = bias_sums[at : at + hidden_bias.shape[0]]
    at += hidden_bias.shape[0]
    output_bias_grad = bias_sums[at:]
    width_start = seq_index * slice_width
    cond_cols = lax.dynamic_slice_in_dim(condition, width_start, slice_width, 1)
    low_cols = lax.dynamic_slice_in_dim(cond_low, width_start, slice_width, 1)
    ada_weight_grad = jnp.einsum(
        "wd,wcf->dcf",
        low_cols.astype(f32),
        mod_all,
        precision=HIGHEST,
        preferred_element_type=f32,
    )
    ada_rows = lax.dynamic_slice_in_dim(ada_weight, width_start, slice_width, 0)
    cond_grad = lax.psum(
        jnp.einsum(
            "wcf,dcf->wd",
            mod_all,
            ada_rows.astype(f32),
            precision=HIGHEST,
            preferred_element_type=f32,
        ),
        "tp",
    )
    silu_pull = jax.vjp(jax.nn.silu, cond_cols)[1]
    class_grad = jnp.einsum(
        "wc,wd->cd",
        label_hot.astype(f32),
        silu_pull(cond_grad)[0],
        precision=HIGHEST,
        preferred_element_type=f32,
    )
    qkv_weight_grad, proj_weight_grad, hidden_weight_grad, output_weight_grad = (
        lax.psum_scatter(qkv_weight_term, "seq", scatter_dimension=0, tiled=True).astype(f32),
        lax.psum_scatter(proj_weight_term, "seq", scatter_dimension=1, tiled=True).astype(f32),
        lax.psum_scatter(hidden_weight_term, "seq", scatter_dimension=0, tiled=True).astype(f32),
        lax.psum_scatter(output_weight_term, "seq", scatter_dimension=1, tiled=True).astype(f32),
    )
    return (
        output,
        tokens_grad,
        class_grad,
        ada_weight_grad,
        ada_bias_grad,
        qkv_weight_grad,
        qv_bias_grad,
        proj_weight_grad,
        proj_bias_grad,
        hidden_weight_grad,
        hidden_bias_grad,
        output_weight_grad,
        output_bias_grad,
    )


def solution(mesh):
    return jax.shard_map(
        local,
        mesh=mesh,
        in_specs=(
            P("seq", "tp"),
            P("seq", "tp"),
            P("seq"),
            P(),
            P(),
            P(),
            P(),
            P(None, None, "tp"),
            P(None, "tp"),
            P(None, None, "tp"),
            P(None, "tp"),
            P("tp", None),
            P("tp"),
            P(None, "tp"),
            P("tp"),
            P("tp", None),
            P("tp"),
        ),
        out_specs=(
            P("seq", "tp"),
            P("seq", "tp"),
            P(None, "seq"),
            P("seq", None, "tp"),
            P(None, "tp"),
            P("seq", None, "tp"),
            P(None, "tp"),
            P("tp", "seq"),
            P("tp"),
            P("seq", "tp"),
            P("tp"),
            P("tp", "seq"),
            P("tp"),
        ),
        check_vma=False,
    )
```

time: 1070 us -> 595 us (0.56)
  waiting for transfers between devices: 671 us -> 324 us
  local copies, waits for them, and re-layouts: 87.5 us -> 24.1 us
  blocking collectives: 105 us -> 75.1 us
  starting transfers between devices: 23.5 us -> 1.08 us
  other arithmetic: 53.5 us -> 33.7 us
  matrix products: 98.7 us -> 117 us
    reduce_scatter x6 -> x4, waiting for transfers between devices: 351 us -> 77.5 us  [column_sum(): lax.psum_scatter(part_rows.astype(bf16), 'tp', scatter_dimension=1, tiled...]
    reduce_scatter x1, waiting for transfers between devices: 108 us -> 13.1 us  [local(): lax.psum_scatter(qkv_weight_term, 'seq', scatter_dimension=0, tiled=True)]
    reduce_scatter x1, waiting for transfers between devices: 0.01 us -> 62.3 us  [local(): lax.psum_scatter(proj_weight_term, 'seq', scatter_dimension=1, tiled=True)]
    psum x2 -> x0, blocking collectives: 53.2 us -> none  [the longest x1 42.5 us: local(): lax.psum((ada_bias_term, qv_bias_term, proj_bias_term, hidden_bias_term,...]
    reduce_scatter x1, waiting for transfers between devices: 108 us -> 71.5 us  [local(): lax.psum_scatter(hidden_weight_term, 'seq', scatter_dimension=0, tiled=True)]
    all_gather x0 -> x1, blocking collectives: none -> 31.7 us  [local(): small_all = lax.all_gather(small, 'seq', axis=0)]
    unnamed x152 -> x94, local copies, waits for them, and re-layouts: 34.1 us -> 4.17 us
    ppermute x8 -> x0, starting transfers between devices: 22.1 us -> none  [the longest x6 16.9 us: passed_along(): return lax.ppermute(array, axis, pairs)]
  transfers between devices with their start and end apart: 22 -> 12, of which waited for: 14 -> 11; matrix products, arithmetic and copies ran while one was open for 15% -> 20% of each run, Pallas kernels for 0% -> 0%
where the time goes in v1:
time: 595 us; the launch traced here: 590 us
  waiting for transfers between devices  324 us (54%)
  matrix products  117 us (20%)
  blocking collectives  75.1 us (13%)
  other arithmetic  33.7 us (6%)
  local copies, waits for them, and re-layouts  24.1 us (4%)
  between operations  15.1 us (3%)
    reduce_scatter x4, waiting for transfers between devices, column_sum(): lax.psum_scatter(part_rows.astype(bf16), 'tp', scatter_dimension=1, tiled...  77.5 us
    reduce_scatter x1, waiting for transfers between devices, local(): lax.psum_scatter(output_weight_term, 'seq', scatter_dimension=1, tiled=True)  71.6 us
    reduce_scatter x1, waiting for transfers between devices, local(): lax.psum_scatter(hidden_weight_term, 'seq', scatter_dimension=0, tiled=True)  71.5 us
    reduce_scatter x1, waiting for transfers between devices, local(): lax.psum_scatter(proj_weight_term, 'seq', scatter_dimension=1, tiled=True)  62.3 us
    all_gather x1, blocking collectives, local(): small_all = lax.all_gather(small, 'seq', axis=0)  31.7 us
    all_gather x4, waiting for transfers between devices, whole_rows(): return lax.all_gather(part_rows, 'tp', axis=1, tiled=True)  27.8 us
    all_gather x1, blocking collectives, local(): mod_full = lax.all_gather(mod_own, 'tp', axis=2, tiled=True)  26.5 us
    dot_general x6, matrix products, exact_dot(): jnp.dot(left_mat, right_mat, precision=HIGHEST, preferred_element_type=jn...  19.7 us
  transfers between devices with their start and end apart: 12, of which 11 were waited for; matrix products, arithmetic and copies ran while one was open for 20% of the time, Pallas kernels for 0%

profile of v1, /device:TPU:0, one launch (start us, length us, event | category | flops | bytes accessed | tf_op | source)
XLA Modules:
  0.0 589.7 jit_solution(4795627765267242598)
XLA Ops:
  21.1 26.5 %all_gather.22 = f32[4,6,1152]{1,0,2:T(4,128)S(1)} all-gather(f32[4,6,288]{1,0,2:T(4,128)S(1)} %copy.102), channel_id=1, replica_groups=mesh['seq'=8,'tp'=4] {'tp'}, dimensions={2}, use_global_device_ids=true | all-gather | bytes 138240 | tf_op jit(solution)/shard_map/all_gather | solution.py:105
  47.6 6.0 %fusion.109 = (f32[4,1,1152]{1,0,2:T(4,128)}, f32[4,1,1152]{1,0,2:T(4,128)}, f32[4,1,1152]{1,0,2:T(4,128)}, f32[4,1,1152]{1,0,2:T(4,128)}) fusion(f32[4,6,1152]{1,0,2:T(4,128)S(1)} %all_gather.22), kind=kLoop, calls=%fused_computation.184 | loop fusion | bytes 147456 | tf_op jit(solution)/shard_map/slice | solution.py:108
  73.1 6.5 %fusion.113 = (f32[4,640]{1,0:T(4,128)S(1)}, f32[4,640,640]{1,2,0:T(8,128)}) fusion(pred[640,640]{0,1:T(8,128)(4,1)} %broadcast_compare_fusion, bf16[640,4,72]{0,2,1:T(8,128)(2,1)S(1)} %bitcast.99, bf16[640,4,72]{0,2,1:T(8,128)(2,1)S(1)} %bitcast.97), kind=kOutput, calls=%fused_computation.188 | convolution fusion | flops 242483840 | bytes 7710720 | tf_op jit(solution)/shard_map/sub | solution.py:155
  89.1 25.1 %reduce-scatter.9.cloned.1.call-done = bf16[640,288]{0,1:T(8,128)(2,1)} async-done(((bf16[640,1152]{0,1:T(8,128)(2,1)}), bf16[640,288]{0,1:T(8,128)(2,1)}) %reduce-scatter.9.cloned.1.call-update) | async-done | bytes 368656 | tf_op jit(solution)/shard_map/reduce_scatter | solution.py:82
  124.7 10.9 %all-gather.10.cloned.1.call-done = bf16[640,1152]{0,1:T(8,128)(2,1)} async-done(((bf16[640,288]{0,1:T(8,128)(2,1)}), bf16[640,1152]{0,1:T(8,128)(2,1)}) %all-gather.10.cloned.1.call-update) | async-done | bytes 1474576 | tf_op jit(solution)/shard_map/all_gather | solution.py:79
  135.6 6.1 %fusion.115 = f32[640,1152]{0,1:T(8,128)} fusion(bf16[1152,1152]{1,0:T(8,128)(2,1)} %param.32, bf16[640,1152]{0,1:T(8,128)(2,1)} %all-gather.10.cloned.1.call-done), kind=kOutput, calls=%fused_computation.190 | convolution fusion | flops 1698693120 | bytes 7077888 | tf_op jit(solution)/shard_map/rd,fd->rf/dot_general | solution.py:185
  141.7 15.1 %all-gather.8.cloned.1.call-done = bf16[640,1152]{0,1:T(8,128)(2,1)} async-done(((bf16[640,288]{0,1:T(8,128)(2,1)}), bf16[640,1152]{0,1:T(8,128)(2,1)}) %all-gather.8.cloned.1.call-update) | async-done | bytes 1474576 | tf_op jit(solution)/shard_map/all_gather | solution.py:79
  160.4 3.9 fusion.11
  164.4 6.0 %convert_reduce_fusion.2 = (f32[1152]{0:T(1024)S(1)}, bf16[640,1152]{0,1:T(8,128)(2,1)S(1)}, f32[640,1152]{0,1:T(8,128)}) fusion(f32[640,1152]{0,1:T(8,128)S(1)} %copy-done.43, f32[1152]{0:T(1024)S(1)} %convert_element_type.178, bf16[640,1152]{0,1:T(8,128)(2,1)S(1)} %fusion.11, bf16[1152,1152]{1,0:T(8,128)(2,1)S(1)} %copy-done), kind=kOutput, calls=%fused_computation.42 | convolution fusion | flops 1715649408 | bytes 11510784 | tf_op jit(solution)/shard_map/dot_general | solution.py:171
  178.8 24.3 %reduce-scatter.13.cloned.1.call-done = bf16[640,288]{0,1:T(8,128)(2,1)} async-done(((bf16[640,1152]{0,1:T(8,128)(2,1)}), bf16[640,288]{0,1:T(8,128)(2,1)}) %reduce-scatter.13.cloned.1.call-update) | async-done | bytes 368656 | tf_op jit(solution)/shard_map/reduce_scatter | solution.py:82
  204.5 5.9 all-reduce.1
  213.4 6.6 %convolution_convert_fusion.4 = bf16[640,1152]{0,1:T(8,128)(2,1)} fusion(bf16[1152,1152]{1,0:T(8,128)(2,1)} %param.32, f32[640,1152]{0,1:T(8,128)} %get-tuple-element.54), kind=kOutput, calls=%fused_computation.28 | convolution fusion | flops 1706065920 | bytes 7077888 | tf_op jit(solution)/shard_map/dot_general | solution.py:176
  220.0 5.4 convolution_convert_fusion.1
  225.5 5.8 convolution_convert_fusion
  238.1 4.1 multiply_reduce_fusion
  248.0 4.3 fusion.41
  257.8 5.6 convolution_convert_fusion.2
  267.4 71.5 %reduce-scatter.21.cloned.1.call-done = bf16[144,1152]{1,0:T(8,128)(2,1)} async-done(((bf16[1152,1152]{1,0:T(8,128)(2,1)}), bf16[144,1152]{1,0:T(8,128)(2,1)}) %reduce-scatter.21.cloned.1.call-update) | async-done | bytes 331792 | tf_op jit(solution)/shard_map/reduce_scatter | solution.py:303
  340.7 71.6 %reduce-scatter.23.cloned.1.call-done = bf16[1152,144]{0,1:T(8,128)(2,1)} async-done(((bf16[1152,1152]{0,1:T(8,128)(2,1)}), bf16[1152,144]{0,1:T(8,128)(2,1)}) %reduce-scatter.23.cloned.1.call-update) | async-done | bytes 331792 | tf_op jit(solution)/shard_map/reduce_scatter | solution.py:304
  414.1 62.3 %reduce-scatter.19.cloned.1.call-done = bf16[288,144]{0,1:T(8,128)(2,1)} async-done(((bf16[288,1152]{0,1:T(8,128)(2,1)}), bf16[288,144]{0,1:T(8,128)(2,1)}) %reduce-scatter.19.cloned.1.call-update) | async-done | bytes 82960 | tf_op jit(solution)/shard_map/reduce_scatter | solution.py:302
  478.1 27.7 %reduce-scatter.15.cloned.1.call-done = bf16[640,288]{0,1:T(8,128)(2,1)} async-done(((bf16[640,1152]{0,1:T(8,128)(2,1)}), bf16[640,288]{0,1:T(8,128)(2,1)}) %reduce-scatter.15.cloned.1.call-update) | async-done | bytes 368656 | tf_op jit(solution)/shard_map/reduce_scatter | solution.py:82
  512.5 31.7 %all-gather = f32[73728]{0:T(1024)S(1)} all-gather(f32[9216]{0:T(1024)S(1)} %concatenate.21), channel_id=2, replica_groups=mesh['seq'=8,'tp'=4] {'seq'}, dimensions={0}, use_global_device_ids=true | all-gather | bytes 331776 | tf_op jit(solution)/shard_map/all_gather | solution.py:259
  548.6 11.0 %all-reduce = (f32[640]{0:T(1024)S(1)}, f32[640]{0:T(1024)S(1)}, f32[32,144]{1,0:T(8,128)S(1)}) all-reduce(f32[640]{0:T(1024)S(1)} %broadcast_multiply_fusion, f32[640]{0:T(1024)S(1)} %broadcast_multiply_fusion.1, f32[32,144]{1,0:T(8,128)S(1)} %convolution_bitcast_fusion.1), channel_id=1, replica_groups=mesh['seq'=8,'tp'=4] {'tp'}, use_global_device_ids=true, to_apply=%region_22.23 | all-reduce | flops 5888 | bytes 47104 | tf_op jit(solution)/shard_map/psum | solution.py:117
  567.7 13.1 %reduce-scatter.17.cloned.1.call-done = bf16[144,3,288]{2,0,1:T(8,128)(2,1)} async-done(((bf16[1152,3,288]{2,0,1:T(8,128)(2,1)}), bf16[144,3,288]{2,0,1:T(8,128)(2,1)}) %reduce-scatter.17.cloned.1.call-update) | async-done | bytes 248848 | tf_op jit(solution)/shard_map/reduce_scatter | solution.py:301
  (210 shorter events, 117.7 us)
Async XLA Ops:
  7.2 157.2 %copy-start = (bf16[1152,1152]{1,0:T(8,128)(2,1)S(1)}, bf16[1152,1152]{1,0:T(8,128)(2,1)}, u32[]{:S(2)}) copy-start(bf16[1152,1152]{1,0:T(8,128)(2,1)} %param.30) | copy-start | bytes 7962628
  7.2 55.6 %all-gather.6.cloned.1.call-start = ((), (), s32[]{:S(2)}) async-start(), calls=%async_computation.8 | async-start | bytes 1843200 | tf_op jit(solution)/shard_map/all_gather | solution.py:79
  13.7 100.5 %reduce-scatter.9.cloned.1.call-start = ((), (), s32[]{:S(2)}) async-start(), calls=%async_computation.9 | async-start | bytes 1843200 | tf_op jit(solution)/shard_map/reduce_scatter | solution.py:82
  73.1 6.5 %copy-start.16 = (bf16[640,1,288]{0,2,1:T(8,128)(2,1)}, bf16[640,1,288]{0,2,1:T(8,128)(2,1)S(1)}, u32[]{:S(2)}) copy-start(bf16[640,1,288]{0,2,1:T(8,128)(2,1)S(1)} %get-tuple-element.38) | copy-start | bytes 1105924
  73.1 6.5 %copy-start.17 = (bf16[640,1,288]{0,2,1:T(8,128)(2,1)}, bf16[640,1,288]{0,2,1:T(8,128)(2,1)S(1)}, u32[]{:S(2)}) copy-start(bf16[640,1,288]{0,2,1:T(8,128)(2,1)S(1)} %get-tuple-element.39) | copy-start | bytes 1105924
  86.2 31.0 %copy-start.28 = (bf16[1152]{0:T(1024)(128)(2,1)S(1)}, bf16[1152]{0:T(1024)(128)(2,1)}, u32[]{:S(2)}) copy-start(bf16[1152]{0:T(1024)(128)(2,1)} %param.31) | copy-start | bytes 6916
  86.2 49.3 %all-gather.10.cloned.1.call-start = ((), (), s32[]{:S(2)}) async-start(), calls=%async_computation.12 | async-start | bytes 1843200 | tf_op jit(solution)/shard_map/all_gather | solution.py:79
  89.0 67.8 %all-gather.8.cloned.1.call-start = ((), (), s32[]{:S(2)}) async-start(), calls=%async_computation.10 | async-start | bytes 1843200 | tf_op jit(solution)/shard_map/all_gather | solution.py:79
  117.1 85.9 %reduce-scatter.13.cloned.1.call-start = ((), (), s32[]{:S(2)}) async-start(), calls=%async_computation.13 | async-start | bytes 1843200 | tf_op jit(solution)/shard_map/reduce_scatter | solution.py:82
  175.3 27.7 %copy-start.5 = (f32[640,1152]{0,1:T(8,128)S(1)}, f32[640,1152]{0,1:T(8,128)}, u32[]{:S(2)}) copy-start(f32[640,1152]{0,1:T(8,128)} %fusion.57) | copy-start | bytes 8847364
  175.4 58.3 %all-gather.12.cloned.1.call-start = ((), (), s32[]{:S(2)}) async-start(), calls=%async_computation.14 | async-start | bytes 1843200 | tf_op jit(solution)/shard_map/all_gather | solution.py:79
  213.3 50.6 %reduce-scatter.11.cloned.1.call-start = ((), (), s32[]{:S(2)}) async-start(), calls=%async_computation.11 | async-start | bytes 1843200 | tf_op jit(solution)/shard_map/reduce_scatter | solution.py:82
  213.3 6.7 %copy-start.13 = (bf16[640,1152]{0,1:T(8,128)(2,1)S(1)}, bf16[640,1152]{0,1:T(8,128)(2,1)}, u32[]{:S(2)}) copy-start(bf16[640,1152]{0,1:T(8,128)(2,1)} %copy-done.12) | copy-start | bytes 4423684
  220.0 118.9 %reduce-scatter.21.cloned.1.call-start = ((), (), s32[]{:S(2)}) async-start(), calls=%async_computation.18 | async-start | bytes 2985984 | tf_op jit(solution)/shard_map/reduce_scatter | solution.py:303
  225.5 186.8 %reduce-scatter.23.cloned.1.call-start = ((), (), s32[]{:S(2)}) async-start(), calls=%async_computation.19 | async-start | bytes 2985984 | tf_op jit(solution)/shard_map/reduce_scatter | solution.py:304
  231.4 245.1 %reduce-scatter.19.cloned.1.call-start = ((), (), s32[]{:S(2)}) async-start(), calls=%async_computation.17 | async-start | bytes 995328 | tf_op jit(solution)/shard_map/reduce_scatter | solution.py:302
  246.2 259.5 %reduce-scatter.15.cloned.1.call-start = ((), (), s32[]{:S(2)}) async-start(), calls=%async_computation.15 | async-start | bytes 1843200 | tf_op jit(solution)/shard_map/reduce_scatter | solution.py:82
  255.6 325.2 %reduce-scatter.17.cloned.1.call-start = ((), (), s32[]{:S(2)}) async-start(), calls=%async_computation.16 | async-start | bytes 2985984 | tf_op jit(solution)/shard_map/reduce_scatter | solution.py:301
  257.8 6.1 %copy-start.10 = (f32[640,288]{0,1:T(8,128)S(1)}, f32[640,288]{0,1:T(8,128)}, u32[]{:S(2)}) copy-start(f32[640,288]{0,1:T(8,128)} %get-tuple-element.52) | copy-start | bytes 2211844
  257.8 6.1 %copy-start.14 = (bf16[640,288]{0,1:T(8,128)(2,1)S(1)}, bf16[640,288]{0,1:T(8,128)(2,1)}, u32[]{:S(2)}) copy-start(bf16[640,288]{0,1:T(8,128)(2,1)} %reduce-scatter.9.cloned.1.call-done) | copy-start | bytes 1105924
  267.3 241.1 %copy-start.9 = (f32[640,288]{0,1:T(8,128)S(1)}, f32[640,288]{0,1:T(8,128)}, u32[]{:S(2)}) copy-start(f32[640,288]{0,1:T(8,128)} %get-tuple-element.30) | copy-start | bytes 2211844
  414.1 94.4 %copy-start.8 = (bf16[640,288]{0,1:T(8,128)(2,1)S(1)}, bf16[640,288]{0,1:T(8,128)(2,1)}, u32[]{:S(2)}) copy-start(bf16[640,288]{0,1:T(8,128)(2,1)} %reduce-scatter.13.cloned.1.call-done) | copy-start | bytes 1105924
  544.2 20.1 %copy-start.15 = (bf16[640,288]{0,1:T(8,128)(2,1)S(1)}, bf16[640,288]{0,1:T(8,128)(2,1)}, u32[]{:S(2)}) copy-start(bf16[640,288]{0,1:T(8,128)(2,1)} %reduce-scatter.15.cloned.1.call-done) | copy-start | bytes 1105924
  562.4 20.3 %copy-start.1 = (bf16[1152,1152]{1,0:T(8,128)(2,1)S(1)}, bf16[1152,1152]{1,0:T(8,128)(2,1)}, u32[]{:S(2)}) copy-start(bf16[1152,1152]{1,0:T(8,128)(2,1)} %param.30) | copy-start | bytes 7962628
  (35 other events, 128.6 us)
Sparse Core Ops, SparseCore 0:
  13.8 29.6 all-gather.5
  86.4 27.8 reduce-scatter.8
  116.4 19.1 all-gather.9
  137.7 19.0 all-gather.7
  175.5 27.5 reduce-scatter.12
  213.4 20.2 all-gather.11
  236.2 27.5 reduce-scatter.10
  268.0 70.8 reduce-scatter.20
  342.5 69.7 reduce-scatter.22
  416.5 59.9 reduce-scatter.18
  479.2 26.4 reduce-scatter.14
  509.2 71.5 reduce-scatter.16
